TPU v7x, 32 devices: a whole 2x2x4 slice. The times are simulated.
32 devices in a mesh: groups: 2 (over y), seq: 4 (over z), dp: 2 (over x), mp: 2 (over core).
Axes of the slice: x: 2, y: 2, z: 4, core: 2. Of those that a mesh axis runs over, the one named last changes fastest.
Arguments:
- tiles: bfloat16 [160, 8, 8, 768], P(('groups', 'seq', 'dp')), parts along dimension 0, may hold values from -6 to 6
- token_grad: bfloat16 [160, 8, 8, 768], P(('groups', 'seq', 'dp')), parts along dimension 0, may hold values from -1.5 to 1.5
- embed_grad: bfloat16 [2, 80, 768], P('dp', 'groups', 'seq'), parts along dimension 1, may hold values from -48 to 48
- live_tiles: int32 [16], P(('groups', 'seq', 'dp')), parts along dimension 0, may hold values from 1 to 10, 60 in all
- dw_kernel: float32 [7, 7, 768], replicated, may hold values from -0.875 to 0.875
- dw_bias: float32 [768], replicated, may hold values from -3 to 3
- ln_gain: float32 [768], replicated, may hold values from 0.1 to 1.9
- ln_bias: float32 [768], replicated, may hold values from -2 to 2
- w_up: bfloat16 [768, 2560], P('seq', 'mp'), may hold values from -0.21875 to 0.21875
- b_up: float32 [2560], P('mp'), may hold values from -3 to 3
- w_down: bfloat16 [768, 2560], P('seq', 'mp'), may hold values from -0.125 to 0.125
- layer_scale: float32 [768], replicated, may hold values from 0.3 to 1.5
Outputs:
- tile_grad: bfloat16 [160, 8, 8, 768], P(('groups', 'seq', 'dp')), parts along dimension 0
- grad_up: float32 [1536, 2560], P(('groups', 'seq'), 'mp'), parts along dimension 0
- grad_down: float32 [1536, 2560], P(('groups', 'seq'), 'mp'), parts along dimension 0
There are 2 independent parts, one for each index of `groups`. A program takes and returns all parts, laid end to end along the dimension named above; an argument that names none is the same for every part. Nothing has to cross between parts.
Inputs may be any that keep to these rules, and one draw needn't show every extreme that they name: Each loader's foreground tiles fill its slots 0 to live_tiles - 1 of 10; some loader has all 10.
All inputs are finite; a program needn't handle non-finite values. No bound on the sum of `live_tiles` on one device may be relied on, other than what follows from the above.
Results may differ from a plain program's by a relative error of at most 0.01.
Values may be sent and summed in bfloat16 or wider, within the bound.
No kernel may reach another device: no remote copies, remote signals or barrier semaphores. Data moves between devices by JAX's collectives and lax.ppermute only.
A program may use at most 64 MiB of HBM per device.

v0:
```python
import jax
import jax.numpy as jnp
from jax import lax
from jax.sharding import PartitionSpec as P

sqrt_two_pi = 0.7978845608028654
cubic_coef = 0.044715


def depthwise(values, kernel):
    reach = kernel.shape[0]
    margin = reach // 2
    height = values.shape[1]
    padded = jnp.pad(values, ((0, 0), (margin, margin), (margin, margin), (0, 0)))
    total = jnp.zeros(values.shape, jnp.float32)
    for row_off in range(reach):
        for col_off in range(reach):
            total = (
                total
                + padded[:, row_off : row_off + height, col_off : col_off + height, :]
                * kernel[row_off, col_off]
            )
    return total


def gelu_tanh(values):
    inner = sqrt_two_pi * (values + cubic_coef * values * values * values)
    return 0.5 * values * (1.0 + jnp.tanh(inner))


def gelu_slope(values):
    tangent = jnp.tanh(sqrt_two_pi * (values + cubic_coef * values * values * values))
    return 0.5 * (1.0 + tangent) + 0.5 * values * (1.0 - tangent * tangent) * sqrt_two_pi * (
        1.0 + 3.0 * cubic_coef * values * values
    )


def normalize(values):
    center = jnp.mean(values, axis=-1, keepdims=True)
    shifted = values - center
    spread = jnp.sqrt(jnp.mean(shifted * shifted, axis=-1, keepdims=True) + 1e-06)
    return (shifted / spread, spread)


def norm_backward(normed_grad, normal, spread, ln_gain):
    scaled = normed_grad * ln_gain
    return (
        scaled
        - jnp.mean(scaled, axis=-1, keepdims=True)
        - normal * jnp.mean(scaled * normal, axis=-1, keepdims=True)
    ) / spread


def on_device(
    tiles,
    token_grad,
    embed_grad,
    live_tiles,
    dw_kernel,
    dw_bias,
    ln_gain,
    ln_bias,
    w_up,
    b_up,
    w_down,
    layer_scale,
):
    count = tiles.shape[0]
    height = tiles.shape[1]
    width = tiles.shape[3]
    flipped = dw_kernel[::-1, ::-1, :]
    arrived = lax.all_to_all(embed_grad[0], "seq", split_axis=0, concat_axis=1, tiled=True)
    live = (jnp.arange(count) < live_tiles[0]).astype(jnp.float32)[:, None, None, None]
    pooled = arrived.astype(jnp.float32)[:, None, None, :] * live
    out_grad = live * token_grad.astype(jnp.float32) + pooled / (height * height)
    branch_grad = (layer_scale * out_grad).astype(jnp.bfloat16).reshape(-1, width)
    conv = depthwise(tiles.astype(jnp.float32), dw_kernel) + dw_bias
    normal, spread = normalize(conv)
    normed = (normal * ln_gain + ln_bias).astype(jnp.bfloat16)
    rows = normed.reshape(-1, width)
    full_up, full_down = (
        lax.all_gather(w_up, "seq", axis=0, tiled=True),
        lax.all_gather(w_down, "seq", axis=0, tiled=True),
    )
    hidden = jnp.dot(rows, full_up, preferred_element_type=jnp.float32) + b_up
    act = gelu_tanh(hidden).astype(jnp.bfloat16)
    act_grad = jnp.dot(branch_grad, full_down, preferred_element_type=jnp.float32)
    hidden_grad = (act_grad * gelu_slope(hidden)).astype(jnp.bfloat16)
    normed_part = lax.dot_general(
        hidden_grad, full_up, (((1,), (1,)), ((), ())), preferred_element_type=jnp.float32
    )
    part_down = lax.dot_general(
        branch_grad, act, (((0,), (0,)), ((), ())), preferred_element_type=jnp.float32
    )
    part_up = lax.dot_general(
        rows, hidden_grad, (((0,), (0,)), ((), ())), preferred_element_type=jnp.float32
    )
    up_piece, down_piece = (
        lax.psum_scatter(
            part_up.astype(jnp.bfloat16), "seq", scatter_dimension=0, tiled=True
        ).astype(jnp.float32),
        lax.psum_scatter(
            part_down.astype(jnp.bfloat16), "seq", scatter_dimension=0, tiled=True
        ).astype(jnp.float32),
    )
    grad_up, grad_down = (
        lax.psum(up_piece.astype(jnp.bfloat16), "dp").astype(jnp.float32),
        lax.psum(down_piece.astype(jnp.bfloat16), "dp").astype(jnp.float32),
    )
    normed_grad = lax.psum(normed_part.astype(jnp.bfloat16), "mp").astype(jnp.float32)
    conv_grad = norm_backward(normed_grad.reshape(conv.shape), normal, spread, ln_gain)
    tile_grad = (out_grad + depthwise(conv_grad, flipped)).astype(jnp.bfloat16)
    return (tile_grad, grad_up, grad_down)


def solution(mesh):
    return jax.shard_map(
        on_device,
        mesh=mesh,
        in_specs=(
            P(("groups", "seq", "dp"), None, None, None),
            P(("groups", "seq", "dp"), None, None, None),
            P("dp", "groups", "seq"),
            P(("groups", "seq", "dp")),
            P(),
            P(),
            P(),
            P(),
            P("seq", "mp"),
            P("mp"),
            P("seq", "mp"),
            P(),
        ),
        out_specs=(
            P(("groups", "seq", "dp"), None, None, None),
            P(("groups", "seq"), "mp"),
            P(("groups", "seq"), "mp"),
        ),
        check_vma=False,
    )
```

profile of v0, /device:TPU:0, one launch (start us, length us, event | category | flops | bytes accessed | tf_op | source)
XLA Modules:
  0.0 267.0 jit_solution(10190657379910288535)
XLA Ops:
  7.2 0.0 all-gather.5.cloned.1.call-start
  7.2 0.7 all-gather.5.cloned.1.call-update
  7.9 0.7 all_to_all.10
  8.7 0.7 reshape.223
  9.4 6.5 %all-to-all-start = ((bf16[4,2,960]{2,1,0:T(2,128)(2,1)}), bf16[4,2,960]{2,1,0:T(2,128)(2,1)S(1)}, u32[]{:S(2)}, u32[]{:S(2)}) async-start(bf16[4,2,960]{2,1,0:T(2,128)(2,1)} %reshape.223), calls=%async_computation | async-start | bytes 32768 | tf_op jit(solution)/shard_map/all_to_all | solution.py:72
  15.8 0.7 all-gather.3.cloned.1.call-update
  16.6 0.0 all-reduce.6.cloned.1.call-start
  16.6 1.1 slice_reduce_fusion.46
  17.7 1.4 slice_reduce_fusion.48
  19.1 1.4 slice_reduce_fusion.47
  20.5 0.2 convert_element_type.70
  20.7 13.0 %fusion.209 = (f32[10,8,8]{2,1,0:T(8,128)S(1)}, f32[10,8,8,768]{3,2,1,0:T(8,128)S(1)}) fusion(f32[768]{0:T(1024)S(1)} %copy-done.5, f32[768]{0:T(1024)S(1)} %get-tuple-element.50, f32[768]{0:T(1024)S(1)} %get-tuple-element.51, f32[768]{0:T(1024)S(1)} %get-tuple-element.4, f32[768]{0:T(1024)S(1)} %get-tuple-element.5, f32[768]{0:T(1024)S(1)} %get-tuple-element.6, ...), kind=kLoop, calls=%fused_computation.377 | loop fusion | flops 48659840 | bytes 4088320 | tf_op jit(solution)/shard_map/reduce_sum | solution.py:39
  34.4 0.3 multiply_reduce_fusion.2
  34.7 0.0 copy-start
  34.7 0.0 copy-start.4
  34.7 0.0 copy-done.2
  34.8 1.3 add_convert_fusion
  36.1 0.0 all-to-all-done
  36.1 0.1 reshape.224
  36.3 0.1 reshape.173
  36.4 0.1 multiply_multiply_fusion.1
  36.4 1.3 multiply_convert_fusion.1
  37.7 18.1 %all-gather.5.cloned.1.call-done = bf16[768,1280]{1,0:T(8,128)(2,1)} async-done(((bf16[192,1280]{1,0:T(8,128)(2,1)}), bf16[768,1280]{1,0:T(8,128)(2,1)}) %all-gather.5.cloned.1.call-update) | async-done | bytes 1966096 | tf_op jit(solution)/shard_map/all_gather | solution.py:82
  55.9 5.0 %convolution_add_fusion = f32[640,1280]{1,0:T(8,128)} fusion(bf16[640,768]{1,0:T(8,128)(2,1)} %bitcast.18, bf16[768,1280]{1,0:T(8,128)(2,1)} %all-gather.5.cloned.1.call-done, f32[1280]{0:T(1024)S(1)} %copy-done.7), kind=kOutput, calls=%fused_computation.99 | convolution fusion | flops 1259110400 | bytes 6231040 | tf_op jit(solution)/shard_map/dot_general | solution.py:85
  60.9 39.0 %all-gather.3.cloned.1.call-done = bf16[768,1280]{1,0:T(8,128)(2,1)} async-done(((bf16[192,1280]{1,0:T(8,128)(2,1)}), bf16[768,1280]{1,0:T(8,128)(2,1)}) %all-gather.3.cloned.1.call-update) | async-done | bytes 1966096 | tf_op jit(solution)/shard_map/all_gather | solution.py:83
  99.9 5.7 %fusion.5 = bf16[640,1280]{1,0:T(8,128)(2,1)S(1)} fusion(f32[640,1280]{1,0:T(8,128)} %convolution_add_fusion, bf16[640,768]{1,0:T(8,128)(2,1)} %bitcast.20, bf16[768,1280]{1,0:T(8,128)(2,1)} %all-gather.3.cloned.1.call-done), kind=kOutput, calls=%fused_computation.108 | convolution fusion | flops 1273856000 | bytes 7864320 | tf_op jit(solution)/shard_map/dot_general | solution.py:87
  105.6 1.2 copy-done.8
  106.8 2.4 convolution_convert_fusion.2
  109.2 0.0 all-reduce.6.cloned.1.call-update
  109.2 0.0 reduce-scatter.3.cloned.1.call-start
  109.3 4.8 %convolution_convert_fusion.1 = bf16[768,1280]{1,0:T(8,128)(2,1)} fusion(bf16[640,768]{1,0:T(8,128)(2,1)} %bitcast.19, bf16[640,1280]{1,0:T(8,128)(2,1)} %copy-done.8), kind=kOutput, calls=%fused_computation.101 | convolution fusion | flops 1259274240 | bytes 4587520 | tf_op jit(solution)/shard_map/dot_general | solution.py:95
  114.1 0.0 reduce-scatter.3.cloned.1.call-update
  114.1 0.2 reduce-scatter.5.cloned.1.call-start
  114.3 5.5 %convolution_convert_fusion = bf16[768,1280]{1,0:T(8,128)(2,1)} fusion(bf16[640,768]{1,0:T(8,128)(2,1)} %bitcast.21, f32[640,1280]{1,0:T(8,128)} %convolution_add_fusion), kind=kOutput, calls=%fused_computation.100 | convolution fusion | flops 1266647040 | bytes 6225920 | tf_op jit(solution)/shard_map/dot_general | solution.py:92
  119.9 0.0 reduce-scatter.5.cloned.1.call-update
  119.9 0.0 all-reduce.8.cloned.1.call-start
  119.9 7.8 %all-reduce.6.cloned.1.call-done = bf16[640,768]{1,0:T(8,128)(2,1)} async-done(((bf16[640,768]{1,0:T(8,128)(2,1)}), bf16[640,768]{1,0:T(8,128)(2,1)}) %all-reduce.6.cloned.1.call-update) | async-done | bytes 983056 | tf_op jit(solution)/shard_map/psum | solution.py:110
  127.7 1.5 multiply_reduce_fusion.1
  129.2 0.1 div.41
  129.3 1.8 multiply_reduce_fusion
  131.1 1.9 subtract_divide_fusion
  133.0 39.7 %reduce-scatter.3.cloned.1.call-done = bf16[192,1280]{1,0:T(8,128)(2,1)} async-done(((bf16[768,1280]{1,0:T(8,128)(2,1)}), bf16[192,1280]{1,0:T(8,128)(2,1)}) %reduce-scatter.3.cloned.1.call-update) | async-done | bytes 491536 | tf_op jit(solution)/shard_map/reduce_scatter | solution.py:99
  172.7 43.0 %reduce-scatter.5.cloned.1.call-done = bf16[192,1280]{1,0:T(8,128)(2,1)} async-done(((bf16[768,1280]{1,0:T(8,128)(2,1)}), bf16[192,1280]{1,0:T(8,128)(2,1)}) %reduce-scatter.5.cloned.1.call-update) | async-done | bytes 491536 | tf_op jit(solution)/shard_map/reduce_scatter | solution.py:102
  215.6 0.0 all-reduce.8.cloned.1.call-update
  215.7 38.3 %fusion.200 = bf16[10,8,8,768]{3,2,1,0:T(8,128)(2,1)} fusion(f32[10,8,8,768]{3,2,1,0:T(8,128)} %subtract_divide_fusion, bf16[10,8,8,768]{3,2,1,0:T(8,128)(2,1)S(1)} %copy-done, f32[768]{0:T(1024)S(1)} %get-tuple-element.50, f32[768]{0:T(1024)S(1)} %get-tuple-element.51, f32[768]{0:T(1024)S(1)} %get-tuple-element.4, f32[768]{0:T(1024)S(1)} %get-tuple-element.5, ...), kind=kLoop, calls=%fused_computation.310 | loop fusion | flops 50135040 | bytes 4113448 | tf_op jit(solution)/shard_map/convert_element_type | solution.py:112
  254.0 2.1 all-reduce.8.cloned.1.call-done
  256.1 2.0 convert_element_type.77
  258.1 2.0 convert_element_type.80
  (22 shorter events, 0.1 us)
Async XLA Ops:
  7.2 13.3 %copy-start.1 = (bf16[10,8,8,768]{3,2,1,0:T(8,128)(2,1)S(1)}, bf16[10,8,8,768]{3,2,1,0:T(8,128)(2,1)}, u32[]{:S(2)}) copy-start(bf16[10,8,8,768]{3,2,1,0:T(8,128)(2,1)} %param.12) | copy-start | bytes 2949124
  7.2 48.7 %all-gather.5.cloned.1.call-start = ((), (), s32[]{:S(2)}) async-start(), calls=%async_computation.4 | async-start | bytes 2457600 | tf_op jit(solution)/shard_map/all_gather | solution.py:82
  9.4 11.3 %copy-start.5 = (f32[768]{0:T(1024)S(1)}, f32[768]{0:T(1024)}, u32[]{:S(2)}) copy-start(f32[768]{0:T(1024)} %param.17) | copy-start | bytes 9220
  9.4 26.7 %all-to-all-start = ((bf16[4,2,960]{2,1,0:T(2,128)(2,1)}), bf16[4,2,960]{2,1,0:T(2,128)(2,1)S(1)}, u32[]{:S(2)}, u32[]{:S(2)}) async-start(bf16[4,2,960]{2,1,0:T(2,128)(2,1)} %reshape.223), calls=%async_computation | async-start | bytes 32768 | tf_op jit(solution)/shard_map/all_to_all | solution.py:72
  15.8 84.0 %all-gather.3.cloned.1.call-start = ((), (), s32[]{:S(2)}) async-start(), calls=%async_computation.3 | async-start | bytes 2457600 | tf_op jit(solution)/shard_map/all_gather | solution.py:83
  16.6 111.2 %all-reduce.6.cloned.1.call-start = ((), (), s32[]{:S(2)}) async-start(), calls=%async_computation.5 | async-start | bytes 1966080 | tf_op jit(solution)/shard_map/psum | solution.py:110
  33.6 1.1 copy-start.2
  33.7 1.1 copy-start.3
  34.7 1.7 copy-start
  34.7 1.7 copy-start.4
  36.1 19.8 %copy-start.7 = (f32[1280]{0:T(1024)S(1)}, f32[1280]{0:T(1024)}, u32[]{:S(2)}) copy-start(f32[1280]{0:T(1024)} %param.21) | copy-start | bytes 15364
  99.9 6.9 %copy-start.6 = (bf16[768,1280]{1,0:T(8,128)(2,1)S(1)}, bf16[768,1280]{1,0:T(8,128)(2,1)}, u32[]{:S(2)}) copy-start(bf16[768,1280]{1,0:T(8,128)(2,1)} %all-gather.5.cloned.1.call-done) | copy-start | bytes 5898244
  105.5 1.2 copy-start.8
  109.2 63.4 %reduce-scatter.3.cloned.1.call-start = ((), (), s32[]{:S(2)}) async-start(), calls=%async_computation.6 | async-start | bytes 2457600 | tf_op jit(solution)/shard_map/reduce_scatter | solution.py:99
  114.1 101.5 %reduce-scatter.5.cloned.1.call-start = ((), (), s32[]{:S(2)}) async-start(), calls=%async_computation.7 | async-start | bytes 2457600 | tf_op jit(solution)/shard_map/reduce_scatter | solution.py:102
  119.9 136.2 %all-reduce.8.cloned.1.call-start = ((), (), s32[]{:S(2)}) async-start(), calls=%async_computation.8 | async-start | bytes 1966080 | tf_op jit(solution)/shard_map/psum | solution.py:107
Sparse Core Ops, SparseCore 0:
  9.6 46.2 all-gather.4
  57.4 42.3 all-gather.2
  109.3 18.3 all-reduce.5
  130.0 42.6 reduce-scatter.2
  174.9 40.6 reduce-scatter.4
  218.0 38.0 all-reduce.7
where the time goes:
time: 268 us; the launch traced here: 267 us
  waiting for transfers between devices  151 us (56%)
  other arithmetic  63.8 us (24%)
  matrix products  23.4 us (9%)
  between operations  14.9 us (6%)
  local copies, waits for them, and re-layouts  6.86 us (3%)
  starting transfers between devices  6.85 us (3%)
    reduce_scatter x1, waiting for transfers between devices, on_device(): lax.psum_scatter(part_down.astype(jnp.bfloat16), 'seq', scatter_dimension...  43 us
    reduce_scatter x1, waiting for transfers between devices, on_device(): lax.psum_scatter(part_up.astype(jnp.bfloat16), 'seq', scatter_dimension=0...  39.7 us
    all_gather x1, waiting for transfers between devices, on_device(): lax.all_gather(w_down, 'seq', axis=0, tiled=True)  39 us
    convert_element_type x1, other arithmetic, on_device(): tile_grad = (out_grad + depthwise(conv_grad, flipped)).astype(jnp.bfloat16)  38.3 us
    all_gather x1, waiting for transfers between devices, on_device(): lax.all_gather(w_up, 'seq', axis=0, tiled=True)  18.1 us
    reduce_sum x1, other arithmetic, normalize(): center = jnp.mean(values, axis=-1, keepdims=True)  13 us
    psum x1, waiting for transfers between devices, on_device(): lax.psum(normed_part.astype(jnp.bfloat16), 'mp').astype(jnp.float32)  7.78 us
    all_to_all x1, starting transfers between devices, on_device(): lax.all_to_all(embed_grad[0], 'seq', split_axis=0, concat_axis=1, tiled=T...  6.46 us
  transfers between devices with their start and end apart: 7, of which 6 were waited for; matrix products, arithmetic and copies ran while one was open for 30% of the time, Pallas kernels for 0%

commit v1 on v0

--- a/solution.py
+++ b/solution.py
@@ -5,6 +5,28 @@
 
 sqrt_two_pi = 0.7978845608028654
 cubic_coef = 0.044715
+
+
+def joined_along(blocks, dim):
+    lengths = list(blocks.shape[1:])
+    lengths[dim] *= blocks.shape[0]
+    return jnp.moveaxis(blocks, 0, dim).reshape(lengths)
+
+
+def ring_gather(shard, axis, dim):
+    peers = lax.axis_size(axis)
+    pairs = [(i, (i + 1) % peers) for i in range(peers)]
+    back = [(b, a) for a, b in pairs]
+    lower, upper = ([], [])
+    for step in range(peers - 1):
+        if step % 2 == 0:
+            lower.append(lax.ppermute(lower[-1] if lower else shard, axis, pairs))
+        else:
+            upper.append(lax.ppermute(upper[-1] if upper else shard, axis, back))
+    pieces = jnp.stack([*lower[::-1], shard, *upper])
+    shift = lax.axis_index(axis) - len(lower)
+    pieces = pieces[(jnp.arange(peers) - shift) % peers]
+    return joined_along(pieces, dim)
 
 
 def depthwise(values, kernel):
@@ -79,7 +101,7 @@
     normed = (normal * ln_gain + ln_bias).astype(jnp.bfloat16)
     rows = normed.reshape(-1, width)
     full_up, full_down = (
-        lax.all_gather(w_up, "seq", axis=0, tiled=True),
+        ring_gather(w_up, "seq", 0),
         lax.all_gather(w_down, "seq", axis=0, tiled=True),
     )
     hidden = jnp.dot(rows, full_up, preferred_element_type=jnp.float32) + b_up

time: 268 us -> 257 us (0.959)
  waiting for transfers between devices: 151 us -> 120 us
  other arithmetic: 63.8 us -> 71.6 us
  local copies, waits for them, and re-layouts: 6.86 us -> 14.4 us
  starting transfers between devices: 6.85 us -> 9.8 us
    all_gather x1, waiting for transfers between devices: 39 us -> 0.01 us  [on_device(): lax.all_gather(w_down, 'seq', axis=0, tiled=True)]
    all_gather x1 -> x0, waiting for transfers between devices: 18.1 us -> none  [on_device(): lax.all_gather(w_up, 'seq', axis=0, tiled=True)]
    ppermute x0 -> x3, waiting for transfers between devices: none -> 15.1 us  [the longest x2 15.1 us: ring_gather(): lower.append(lax.ppermute(lower[-1] if lower else shard, axis, pairs))]
    all_to_all x1, waiting for transfers between devices: 0.01 us -> 14.6 us  [on_device(): lax.all_to_all(embed_grad[0], 'seq', split_axis=0, concat_axis=1, tiled=T...]
    ppermute x0 -> x3, starting transfers between devices: none -> 5.57 us  [the longest x2 3.47 us: ring_gather(): lower.append(lax.ppermute(lower[-1] if lower else shard, axis, pairs))]
    gather x0 -> x1, local copies, waits for them, and re-layouts: none -> 3.66 us  [ring_gather(): pieces = pieces[(jnp.arange(peers) - shift) % peers]]
    reduce_scatter x1, waiting for transfers between devices: 43 us -> 39.4 us  [on_device(): lax.psum_scatter(part_down.astype(jnp.bfloat16), 'seq', scatter_dimension...]
    reduce_scatter x1, waiting for transfers between devices: 39.7 us -> 43 us  [on_device(): lax.psum_scatter(part_up.astype(jnp.bfloat16), 'seq', scatter_dimension=0...]
  transfers between devices with their start and end apart: 7 -> 9, of which waited for: 6 -> 6; matrix products, arithmetic and copies ran while one was open for 30% -> 37% of each run, Pallas kernels for 0% -> 0%
where the time goes in v1:
time: 257 us; the launch traced here: 256 us
  waiting for transfers between devices  120 us (47%)
  other arithmetic  71.6 us (28%)
  matrix products  23.5 us (9%)
  between operations  15.8 us (6%)
  local copies, waits for them, and re-layouts  14.4 us (6%)
  starting transfers between devices  9.8 us (4%)
    reduce_scatter x1, waiting for transfers between devices, on_device(): lax.psum_scatter(part_up.astype(jnp.bfloat16), 'seq', scatter_dimension=0...  43 us
    convert_element_type x1, other arithmetic, on_device(): tile_grad = (out_grad + depthwise(conv_grad, flipped)).astype(jnp.bfloat16)  39.8 us
    reduce_scatter x1, waiting for transfers between devices, on_device(): lax.psum_scatter(part_down.astype(jnp.bfloat16), 'seq', scatter_dimension...  39.4 us
    ppermute x2, waiting for transfers between devices, ring_gather(): lower.append(lax.ppermute(lower[-1] if lower else shard, axis, pairs))  15.1 us
    all_to_all x1, waiting for transfers between devices, on_device(): lax.all_to_all(embed_grad[0], 'seq', split_axis=0, concat_axis=1, tiled=T...  14.6 us
    reduce_sum x1, other arithmetic, normalize(): center = jnp.mean(values, axis=-1, keepdims=True)  12.8 us
    psum x1, waiting for transfers between devices, on_device(): lax.psum(normed_part.astype(jnp.bfloat16), 'mp').astype(jnp.float32)  8.04 us
    dot_general x1, matrix products, on_device(): jnp.dot(branch_grad, full_down, preferred_element_type=jnp.float32)  5.67 us
  transfers between devices with their start and end apart: 9, of which 6 were waited for; matrix products, arithmetic and copies ran while one was open for 37% of the time, Pallas kernels for 0%

profile of v1, /device:TPU:0, one launch (start us, length us, event | category | flops | bytes accessed | tf_op | source)
XLA Modules:
  0.0 255.6 jit_solution(2880195667865687719)
XLA Ops:
  7.2 0.0 all-gather.2.cloned.1.call-start
  7.2 3.1 %collective-permute-start = (bf16[192,1280]{1,0:T(8,128)(2,1)}, bf16[192,1280]{1,0:T(8,128)(2,1)}, u32[]{:S(2)}, u32[]{:S(2)}) collective-permute-start(bf16[192,1280]{1,0:T(8,128)(2,1)} %param.20), channel_id=1, source_target_pairs={{0,4},{4,8},{8,12},{12,0},{1,5},{5,9},{9,13},{13,1},{2,6},{6,10},{... | collective-permute-start | bytes 1474568 | tf_op jit(solution)/shard_map/ppermute | solution.py:23
  10.3 2.1 collective-permute-start.2
  12.4 0.7 all_to_all.10
  13.2 0.7 reshape.284
  13.9 3.8 %all-to-all-start = ((bf16[4,2,960]{2,1,0:T(2,128)(2,1)}), bf16[4,2,960]{2,1,0:T(2,128)(2,1)}, u32[]{:S(2)}, u32[]{:S(2)}) async-start(bf16[4,2,960]{2,1,0:T(2,128)(2,1)} %reshape.284), calls=%async_computation | async-start | bytes 32768 | tf_op jit(solution)/shard_map/all_to_all | solution.py:94
  17.7 0.0 all-reduce.6.cloned.1.call-start
  17.8 1.1 slice_reduce_fusion.46
  19.0 1.4 slice_reduce_fusion.48
  20.6 2.0 slice_reduce_fusion.47
  22.6 1.4 convert_element_type.70
  24.0 12.8 %fusion.211 = (f32[10,8,8]{2,1,0:T(8,128)S(1)}, f32[10,8,8,768]{3,2,1,0:T(8,128)S(1)}) fusion(f32[768]{0:T(1024)S(1)} %copy-done.86, f32[768]{0:T(1024)S(1)} %get-tuple-element.50, f32[768]{0:T(1024)S(1)} %get-tuple-element.51, f32[768]{0:T(1024)S(1)} %get-tuple-element.4, f32[768]{0:T(1024)S(1)} %get-tuple-element.5, f32[768]{0:T(1024)S(1)} %get-tuple-element.6, ...), kind=kLoop, calls=%fused_computation.386 | loop fusion | flops 48659840 | bytes 4088320 | tf_op jit(solution)/shard_map/reduce_sum | solution.py:61
  37.2 0.3 multiply_reduce_fusion.2
  37.6 0.3 copy-done.5
  37.9 0.0 copy-done.85
  37.9 1.3 add_convert_fusion
  39.9 0.6 pad_clamp_fusion
  40.5 0.5 compare_convert_fusion
  41.1 14.6 %all-to-all-done = bf16[4,2,960]{2,1,0:T(2,128)(2,1)} async-done(((bf16[4,2,960]{2,1,0:T(2,128)(2,1)}), bf16[4,2,960]{2,1,0:T(2,128)(2,1)}, u32[]{:S(2)}, u32[]{:S(2)}) %all-to-all-start) | async-done | bytes 15392 | tf_op jit(solution)/shard_map/all_to_all | solution.py:94
  55.6 0.8 reshape.285
  56.4 0.6 copy.16
  57.1 1.5 reshape.226
  58.6 0.4 collective-permute-start.1
  59.0 0.9 multiply_multiply_fusion.1
  59.9 2.0 multiply_convert_fusion.1
  61.9 15.1 %collective-permute-done.1 = bf16[192,1280]{1,0:T(8,128)(2,1)S(1)} collective-permute-done((bf16[192,1280]{1,0:T(8,128)(2,1)}, bf16[192,1280]{1,0:T(8,128)(2,1)S(1)}, u32[]{:S(2)}, u32[]{:S(2)}) %collective-permute-start.1) | collective-permute-done | bytes 491552 | tf_op jit(solution)/shard_map/ppermute | solution.py:23
  77.0 2.7 %pad_maximum_fusion = bf16[4,192,1280]{2,1,0:T(8,128)(2,1)} fusion(bf16[1,192,1280]{2,1,0:T(8,128)(2,1)} %bitcast.7, bf16[1,192,1280]{2,1,0:T(8,128)(2,1)S(1)} %bitcast.31, bf16[1,192,1280]{2,1,0:T(8,128)(2,1)} %bitcast.5, bf16[1,192,1280]{2,1,0:T(8,128)(2,1)S(1)} %bitcast.32), kind=kLoop, calls=%fused_computation.304 | loop fusion | flops 2949120 | bytes 3932160 | tf_op jit(solution)/shard_map/stack | solution.py:26
  79.7 3.7 %gather_fusion = bf16[4,192,1280]{2,1,0:T(8,128)(2,1)} fusion(bf16[4,192,1280]{2,1,0:T(8,128)(2,1)} %pad_maximum_fusion, s32[1024]{0:T(1024)} %pad_clamp_fusion), kind=kCustom, calls=%fused_computation | custom fusion | bytes 3932176 | tf_op jit(solution)/shard_map/gather | solution.py:28
  83.4 5.0 %convolution_add_fusion = f32[640,1280]{1,0:T(8,128)} fusion(bf16[640,768]{1,0:T(8,128)(2,1)} %bitcast.27, bf16[768,1280]{1,0:T(8,128)(2,1)} %bitcast.25, f32[1280]{0:T(1024)S(1)} %copy-done.87), kind=kOutput, calls=%fused_computation.100 | convolution fusion | flops 1259110400 | bytes 6231040 | tf_op jit(solution)/shard_map/dot_general | solution.py:107
  88.5 5.7 %fusion.5 = bf16[640,1280]{1,0:T(8,128)(2,1)S(1)} fusion(f32[640,1280]{1,0:T(8,128)} %convolution_add_fusion, bf16[640,768]{1,0:T(8,128)(2,1)} %bitcast.29, bf16[768,1280]{1,0:T(8,128)(2,1)} %all-gather.2.cloned.1.call-done), kind=kOutput, calls=%fused_computation.109 | convolution fusion | flops 1273856000 | bytes 7864320 | tf_op jit(solution)/shard_map/dot_general | solution.py:109
  94.1 1.2 copy-done.88
  95.3 2.4 convolution_convert_fusion.2
  97.8 0.2 reduce-scatter.5.cloned.1.call-start
  98.0 5.4 %convolution_convert_fusion = bf16[768,1280]{1,0:T(8,128)(2,1)} fusion(bf16[640,768]{1,0:T(8,128)(2,1)} %bitcast.30, f32[640,1280]{1,0:T(8,128)} %convolution_add_fusion), kind=kOutput, calls=%fused_computation.101 | convolution fusion | flops 1266647040 | bytes 6225920 | tf_op jit(solution)/shard_map/dot_general | solution.py:114
  103.5 0.0 reduce-scatter.3.cloned.1.call-start
  103.5 4.9 %convolution_convert_fusion.1 = bf16[768,1280]{1,0:T(8,128)(2,1)} fusion(bf16[640,768]{1,0:T(8,128)(2,1)} %bitcast.28, bf16[640,1280]{1,0:T(8,128)(2,1)} %copy-done.88), kind=kOutput, calls=%fused_computation.102 | convolution fusion | flops 1259274240 | bytes 4587520 | tf_op jit(solution)/shard_map/dot_general | solution.py:117
  108.4 0.0 all-reduce.8.cloned.1.call-start
  108.5 8.0 %all-reduce.6.cloned.1.call-done = bf16[640,768]{1,0:T(8,128)(2,1)} async-done(((bf16[640,768]{1,0:T(8,128)(2,1)}), bf16[640,768]{1,0:T(8,128)(2,1)}) %all-reduce.6.cloned.1.call-update) | async-done | bytes 983056 | tf_op jit(solution)/shard_map/psum | solution.py:132
  116.5 1.5 multiply_reduce_fusion.1
  118.0 0.1 div.41
  118.1 1.8 multiply_reduce_fusion
  120.3 1.9 subtract_divide_fusion
  122.2 39.4 %reduce-scatter.5.cloned.1.call-done = bf16[192,1280]{1,0:T(8,128)(2,1)} async-done(((bf16[768,1280]{1,0:T(8,128)(2,1)}), bf16[192,1280]{1,0:T(8,128)(2,1)}) %reduce-scatter.5.cloned.1.call-update) | async-done | bytes 491536 | tf_op jit(solution)/shard_map/reduce_scatter | solution.py:124
  161.6 43.0 %reduce-scatter.3.cloned.1.call-done = bf16[192,1280]{1,0:T(8,128)(2,1)} async-done(((bf16[768,1280]{1,0:T(8,128)(2,1)}), bf16[192,1280]{1,0:T(8,128)(2,1)}) %reduce-scatter.3.cloned.1.call-update) | async-done | bytes 491536 | tf_op jit(solution)/shard_map/reduce_scatter | solution.py:121
  205.0 39.8 %fusion.200 = bf16[10,8,8,768]{3,2,1,0:T(8,128)(2,1)} fusion(f32[10,8,8,768]{3,2,1,0:T(8,128)} %subtract_divide_fusion, bf16[10,8,8,768]{3,2,1,0:T(8,128)(2,1)S(1)} %copy-done, f32[768]{0:T(1024)S(1)} %copy-done.26, f32[768]{0:T(1024)S(1)} %copy-done.28, f32[768]{0:T(1024)S(1)} %copy-done.32, f32[768]{0:T(1024)S(1)} %copy-done.34, f32[768]{0:T(1024)S(1)} %copy-done.36, ...), kind=kLoop, calls=%fused_computation.312 | loop fusion | flops 50135040 | bytes 4113448 | tf_op jit(solution)/shard_map/convert_element_type | solution.py:134
  244.8 0.2 all-reduce.8.cloned.1.call-done
  245.0 2.0 convert_element_type.77
  247.0 2.0 convert_element_type.80
  (189 shorter events, 0.5 us)
Async XLA Ops:
  7.2 81.3 %all-gather.2.cloned.1.call-start = ((), (), s32[]{:S(2)}) async-start(), calls=%async_computation.3 | async-start | bytes 2457600 | tf_op jit(solution)/shard_map/all_gather | solution.py:105
  7.2 51.4 %collective-permute-start = (bf16[192,1280]{1,0:T(8,128)(2,1)}, bf16[192,1280]{1,0:T(8,128)(2,1)}, u32[]{:S(2)}, u32[]{:S(2)}) collective-permute-start(bf16[192,1280]{1,0:T(8,128)(2,1)} %param.20), channel_id=1, source_target_pairs={{0,4},{4,8},{8,12},{12,0},{1,5},{5,9},{9,13},{13,1},{2,6},{6,10},{... | collective-permute-start | bytes 1474568 | tf_op jit(solution)/shard_map/ppermute | solution.py:23
  10.3 51.6 %collective-permute-start.2 = (bf16[192,1280]{1,0:T(8,128)(2,1)}, bf16[192,1280]{1,0:T(8,128)(2,1)}, u32[]{:S(2)}, u32[]{:S(2)}) collective-permute-start(bf16[192,1280]{1,0:T(8,128)(2,1)} %param.20), channel_id=1, source_target_pairs={{4,0},{8,4},{12,8},{0,12},{5,1},{9,5},{13,9},{1,13},{6,2},{10,6},{... | collective-permute-start | bytes 1474568 | tf_op jit(solution)/shard_map/ppermute | solution.py:25
  13.9 41.7 %all-to-all-start = ((bf16[4,2,960]{2,1,0:T(2,128)(2,1)}), bf16[4,2,960]{2,1,0:T(2,128)(2,1)}, u32[]{:S(2)}, u32[]{:S(2)}) async-start(bf16[4,2,960]{2,1,0:T(2,128)(2,1)} %reshape.284), calls=%async_computation | async-start | bytes 32768 | tf_op jit(solution)/shard_map/all_to_all | solution.py:94
  17.7 98.8 %all-reduce.6.cloned.1.call-start = ((), (), s32[]{:S(2)}) async-start(), calls=%async_computation.4 | async-start | bytes 1966080 | tf_op jit(solution)/shard_map/psum | solution.py:132
  58.6 18.4 %collective-permute-start.1 = (bf16[192,1280]{1,0:T(8,128)(2,1)}, bf16[192,1280]{1,0:T(8,128)(2,1)S(1)}, u32[]{:S(2)}, u32[]{:S(2)}) collective-permute-start(bf16[192,1280]{1,0:T(8,128)(2,1)} %collective-permute-done), channel_id=1, source_target_pairs={{0,4},{4,8},{8,12},{12,0},{1,5},{5,9},{9,13},{13,1},{2,6},{6,10},{... | collective-permute-start | bytes 1474568 | tf_op jit(solution)/shard_map/ppermute | solution.py:23
  97.8 63.8 %reduce-scatter.5.cloned.1.call-start = ((), (), s32[]{:S(2)}) async-start(), calls=%async_computation.6 | async-start | bytes 2457600 | tf_op jit(solution)/shard_map/reduce_scatter | solution.py:124
  103.5 101.1 %reduce-scatter.3.cloned.1.call-start = ((), (), s32[]{:S(2)}) async-start(), calls=%async_computation.5 | async-start | bytes 2457600 | tf_op jit(solution)/shard_map/reduce_scatter | solution.py:121
  108.4 136.6 %all-reduce.8.cloned.1.call-start = ((), (), s32[]{:S(2)}) async-start(), calls=%async_computation.7 | async-start | bytes 1966080 | tf_op jit(solution)/shard_map/psum | solution.py:129
  119.9 84.7 %copy-start.4 = (f32[10,768]{1,0:T(8,128)S(1)}, f32[10,768]{1,0:T(8,128)}, u32[]{:S(2)}) copy-start(f32[10,768]{1,0:T(8,128)} %copy-done.3) | copy-start | bytes 92164
  119.9 84.7 %copy-start.8 = (f32[768]{0:T(1024)S(1)}, f32[768]{0:T(1024)}, u32[]{:S(2)}) copy-start(f32[768]{0:T(1024)} %copy-done.7) | copy-start | bytes 9220
  119.9 84.7 %copy-start.10 = (f32[768]{0:T(1024)S(1)}, f32[768]{0:T(1024)}, u32[]{:S(2)}) copy-start(f32[768]{0:T(1024)} %copy-done.9) | copy-start | bytes 9220
  119.9 84.7 %copy-start.12 = (f32[768]{0:T(1024)S(1)}, f32[768]{0:T(1024)}, u32[]{:S(2)}) copy-start(f32[768]{0:T(1024)} %copy-done.11) | copy-start | bytes 9220
  119.9 84.7 %copy-start.14 = (f32[768]{0:T(1024)S(1)}, f32[768]{0:T(1024)}, u32[]{:S(2)}) copy-start(f32[768]{0:T(1024)} %copy-done.13) | copy-start | bytes 9220
  119.9 84.7 %copy-start.16 = (f32[768]{0:T(1024)S(1)}, f32[768]{0:T(1024)}, u32[]{:S(2)}) copy-start(f32[768]{0:T(1024)} %copy-done.15) | copy-start | bytes 9220
  119.9 84.7 %copy-start.18 = (f32[768]{0:T(1024)S(1)}, f32[768]{0:T(1024)}, u32[]{:S(2)}) copy-start(f32[768]{0:T(1024)} %copy-done.17) | copy-start | bytes 9220
  119.9 84.7 %copy-start.20 = (f32[768]{0:T(1024)S(1)}, f32[768]{0:T(1024)}, u32[]{:S(2)}) copy-start(f32[768]{0:T(1024)} %copy-done.19) | copy-start | bytes 9220
  119.9 84.7 %copy-start.22 = (f32[768]{0:T(1024)S(1)}, f32[768]{0:T(1024)}, u32[]{:S(2)}) copy-start(f32[768]{0:T(1024)} %copy-done.21) | copy-start | bytes 9220
  120.0 84.7 %copy-start.24 = (f32[768]{0:T(1024)S(1)}, f32[768]{0:T(1024)}, u32[]{:S(2)}) copy-start(f32[768]{0:T(1024)} %copy-done.23) | copy-start | bytes 9220
  120.0 84.7 %copy-start.26 = (f32[768]{0:T(1024)S(1)}, f32[768]{0:T(1024)}, u32[]{:S(2)}) copy-start(f32[768]{0:T(1024)} %copy-done.25) | copy-start | bytes 9220
  120.0 84.7 %copy-start.28 = (f32[768]{0:T(1024)S(1)}, f32[768]{0:T(1024)}, u32[]{:S(2)}) copy-start(f32[768]{0:T(1024)} %copy-done.27) | copy-start | bytes 9220
  120.0 84.7 %copy-start.30 = (f32[768]{0:T(1024)S(1)}, f32[768]{0:T(1024)}, u32[]{:S(2)}) copy-start(f32[768]{0:T(1024)} %copy-done.29) | copy-start | bytes 9220
  120.0 84.7 %copy-start.32 = (f32[768]{0:T(1024)S(1)}, f32[768]{0:T(1024)}, u32[]{:S(2)}) copy-start(f32[768]{0:T(1024)} %copy-done.31) | copy-start | bytes 9220
  120.0 84.7 %copy-start.34 = (f32[768]{0:T(1024)S(1)}, f32[768]{0:T(1024)}, u32[]{:S(2)}) copy-start(f32[768]{0:T(1024)} %copy-done.33) | copy-start | bytes 9220
  120.0 84.7 %copy-start.36 = (f32[768]{0:T(1024)S(1)}, f32[768]{0:T(1024)}, u32[]{:S(2)}) copy-start(f32[768]{0:T(1024)} %copy-done.35) | copy-start | bytes 9220
  120.0 84.7 %copy-start.38 = (f32[768]{0:T(1024)S(1)}, f32[768]{0:T(1024)}, u32[]{:S(2)}) copy-start(f32[768]{0:T(1024)} %copy-done.37) | copy-start | bytes 9220
  120.0 84.7 %copy-start.40 = (f32[768]{0:T(1024)S(1)}, f32[768]{0:T(1024)}, u32[]{:S(2)}) copy-start(f32[768]{0:T(1024)} %copy-done.39) | copy-start | bytes 9220
  120.0 84.7 %copy-start.42 = (f32[768]{0:T(1024)S(1)}, f32[768]{0:T(1024)}, u32[]{:S(2)}) copy-start(f32[768]{0:T(1024)} %copy-done.41) | copy-start | bytes 9220
  120.1 84.7 %copy-start.44 = (f32[768]{0:T(1024)S(1)}, f32[768]{0:T(1024)}, u32[]{:S(2)}) copy-start(f32[768]{0:T(1024)} %copy-done.43) | copy-start | bytes 9220
  120.1 84.7 %copy-start.46 = (f32[768]{0:T(1024)S(1)}, f32[768]{0:T(1024)}, u32[]{:S(2)}) copy-start(f32[768]{0:T(1024)} %copy-done.45) | copy-start | bytes 9220
  120.1 84.7 %copy-start.48 = (f32[768]{0:T(1024)S(1)}, f32[768]{0:T(1024)}, u32[]{:S(2)}) copy-start(f32[768]{0:T(1024)} %copy-done.47) | copy-start | bytes 9220
  120.1 84.7 %copy-start.50 = (f32[768]{0:T(1024)S(1)}, f32[768]{0:T(1024)}, u32[]{:S(2)}) copy-start(f32[768]{0:T(1024)} %copy-done.49) | copy-start | bytes 9220
  120.1 84.7 %copy-start.52 = (f32[768]{0:T(1024)S(1)}, f32[768]{0:T(1024)}, u32[]{:S(2)}) copy-start(f32[768]{0:T(1024)} %copy-done.51) | copy-start | bytes 9220
  120.1 84.7 %copy-start.54 = (f32[768]{0:T(1024)S(1)}, f32[768]{0:T(1024)}, u32[]{:S(2)}) copy-start(f32[768]{0:T(1024)} %copy-done.53) | copy-start | bytes 9220
  120.1 84.7 %copy-start.56 = (f32[768]{0:T(1024)S(1)}, f32[768]{0:T(1024)}, u32[]{:S(2)}) copy-start(f32[768]{0:T(1024)} %copy-done.55) | copy-start | bytes 9220
  120.1 84.7 %copy-start.58 = (f32[768]{0:T(1024)S(1)}, f32[768]{0:T(1024)}, u32[]{:S(2)}) copy-start(f32[768]{0:T(1024)} %copy-done.57) | copy-start | bytes 9220
  120.1 84.7 %copy-start.60 = (f32[768]{0:T(1024)S(1)}, f32[768]{0:T(1024)}, u32[]{:S(2)}) copy-start(f32[768]{0:T(1024)} %copy-done.59) | copy-start | bytes 9220
  120.1 84.7 %copy-start.62 = (f32[768]{0:T(1024)S(1)}, f32[768]{0:T(1024)}, u32[]{:S(2)}) copy-start(f32[768]{0:T(1024)} %copy-done.61) | copy-start | bytes 9220
  120.2 84.7 %copy-start.64 = (f32[768]{0:T(1024)S(1)}, f32[768]{0:T(1024)}, u32[]{:S(2)}) copy-start(f32[768]{0:T(1024)} %copy-done.63) | copy-start | bytes 9220
  120.2 84.7 %copy-start.66 = (f32[768]{0:T(1024)S(1)}, f32[768]{0:T(1024)}, u32[]{:S(2)}) copy-start(f32[768]{0:T(1024)} %copy-done.65) | copy-start | bytes 9220
  120.2 84.7 %copy-start.68 = (f32[768]{0:T(1024)S(1)}, f32[768]{0:T(1024)}, u32[]{:S(2)}) copy-start(f32[768]{0:T(1024)} %copy-done.67) | copy-start | bytes 9220
  120.2 84.7 %copy-start.70 = (f32[768]{0:T(1024)S(1)}, f32[768]{0:T(1024)}, u32[]{:S(2)}) copy-start(f32[768]{0:T(1024)} %copy-done.69) | copy-start | bytes 9220
  120.2 84.7 %copy-start.72 = (f32[768]{0:T(1024)S(1)}, f32[768]{0:T(1024)}, u32[]{:S(2)}) copy-start(f32[768]{0:T(1024)} %copy-done.71) | copy-start | bytes 9220
  120.2 84.7 %copy-start.74 = (f32[768]{0:T(1024)S(1)}, f32[768]{0:T(1024)}, u32[]{:S(2)}) copy-start(f32[768]{0:T(1024)} %copy-done.73) | copy-start | bytes 9220
  120.2 84.7 %copy-start.76 = (f32[768]{0:T(1024)S(1)}, f32[768]{0:T(1024)}, u32[]{:S(2)}) copy-start(f32[768]{0:T(1024)} %copy-done.75) | copy-start | bytes 9220
  120.2 84.7 %copy-start.78 = (f32[768]{0:T(1024)S(1)}, f32[768]{0:T(1024)}, u32[]{:S(2)}) copy-start(f32[768]{0:T(1024)} %copy-done.77) | copy-start | bytes 9220
  120.2 84.7 %copy-start.80 = (f32[768]{0:T(1024)S(1)}, f32[768]{0:T(1024)}, u32[]{:S(2)}) copy-start(f32[768]{0:T(1024)} %copy-done.79) | copy-start | bytes 9220
  120.2 84.7 %copy-start.82 = (f32[768]{0:T(1024)S(1)}, f32[768]{0:T(1024)}, u32[]{:S(2)}) copy-start(f32[768]{0:T(1024)} %copy-done.81) | copy-start | bytes 9220
  (50 other events, 842.0 us)
Sparse Core Ops, SparseCore 0:
  12.5 57.2 all-gather.1
  97.9 18.5 all-reduce.5
  118.9 42.6 reduce-scatter.4
  163.9 40.6 reduce-scatter.2
  206.9 38.0 all-reduce.7
